TPU v7x, 512 devices: a whole 4x8x8 slice. The times are simulated.
512 devices in a mesh: item: 16 (over y, core), user: 32 (over z, x).
Axes of the slice: x: 4, y: 8, z: 8, core: 2. Of those that a mesh axis runs over, the one named last changes fastest.
Arguments:
- item_factors: float32 [32768, 128], P('item')
- tile_lists: int32 [512, 16], P(('item', 'user')), may hold values from 0 to 255, as said below
- tile_weights: bfloat16 [512, 16, 128, 128], P(('item', 'user')), may hold values from 0 to 40
- user_factors: float32 [65536, 128], P(('item', 'user')), may hold values from -6 to 6
Outputs:
- new_factors: float32 [65536, 128], P(('item', 'user'))
Inputs may be any that keep to these rules, and one draw needn't show every extreme that they name: `tile_lists`: item shard s holds tiles s * 16 to (s + 1) * 16 - 1. Among the 16 slots of one device's blocks, at most 2 name tiles of one item shard, and for some shard exactly 2 do; a tile may be named more than once.
All inputs are finite; a program needn't handle non-finite values.
Results may differ from a plain program's by a relative error of at most 0.0024.
Values sent between devices are 32-bit elements; how exact they have to be, the bound alone decides.
No kernel may reach another device: no remote copies, remote signals or barrier semaphores. Data moves between devices by JAX's collectives and lax.ppermute only.
A program may use at most 64 MiB of HBM per device.

v0:
```python
import jax
import jax.numpy as jnp
from jax import lax
from jax.sharding import PartitionSpec as P

ITERS = 4
RIDGE_WEIGHT = 0.1
EPSILON = 1e-06
HIGHEST = lax.Precision.HIGHEST


def apply_system(vectors, tiles, weights, gram):
    scores = jnp.einsum("bur,bkir->bkui", vectors, tiles, precision=HIGHEST)
    spread = jnp.einsum("bkui,bkir->bur", scores * weights, tiles, precision=HIGHEST)
    return (
        spread
        + jnp.einsum("bur,rs->bus", vectors, gram, precision=HIGHEST)
        + RIDGE_WEIGHT * vectors
    )


def conjugate(start, tiles, weights, gram, steps):
    weights = weights.astype(jnp.float32)
    target = jnp.einsum("bkui,bkir->bur", 1.0 + weights, tiles, precision=HIGHEST)
    answer = start
    resid = target - apply_system(start, tiles, weights, gram)
    direction = resid
    norm_now = jnp.sum(resid * resid, axis=-1, keepdims=True)
    for step_index in range(steps):
        image = apply_system(direction, tiles, weights, gram)
        alpha = norm_now / (jnp.sum(direction * image, axis=-1, keepdims=True) + EPSILON)
        answer = answer + alpha * direction
        resid = resid - alpha * image
        norm_next = jnp.sum(resid * resid, axis=-1, keepdims=True)
        direction = resid + norm_next / (norm_now + EPSILON) * direction
        norm_now = norm_next
    return answer


def local(item_factors, tile_lists, tile_weights, user_factors):
    factor_rank = item_factors.shape[1]
    tile_side = tile_weights.shape[-1]
    blocks_here, slots_here = tile_lists.shape
    shard_rows = item_factors.shape[0]
    user_parts = lax.axis_size("user")
    share_rows = shard_rows // user_parts
    piece = lax.dynamic_slice_in_dim(
        item_factors, lax.axis_index("user") * share_rows, share_rows, 0
    )
    partial_gram = jnp.dot(piece.T, piece, precision=HIGHEST, preferred_element_type=jnp.float32)
    gram = lax.psum(partial_gram, ("item", "user"))
    tile_ids = tile_lists.reshape(-1)
    all_rows = lax.all_gather(item_factors, "item", axis=0, tiled=True)
    fetched = all_rows.reshape(-1, tile_side, factor_rank)[tile_ids]
    tiles = fetched.reshape(blocks_here, slots_here, tile_side, factor_rank)
    start = user_factors.reshape(blocks_here, tile_side, factor_rank)
    solved = conjugate(start, tiles, tile_weights, gram, ITERS)
    return solved.reshape(-1, factor_rank)


def solution(mesh):
    in_specs = (
        P("item", None),
        P(("item", "user"), None),
        P(("item", "user"), None, None, None),
        P(("item", "user"), None),
    )
    out_specs = P(("item", "user"), None)
    return jax.shard_map(local, mesh=mesh, in_specs=in_specs, out_specs=out_specs, check_vma=False)
```

profile of v0, /device:TPU:1, one launch (start us, length us, event | category | flops | bytes accessed | tf_op | source)
XLA Modules:
  0.0 362.3 jit_solution(888267724627594206)
XLA Ops:
  7.4 0.7 all-gather.2.cloned.1.call-update
  8.1 1.8 fusion.22
  9.9 0.7 fusion.24
  10.6 1.3 copy.24
  11.9 0.9 copy.33
  12.8 101.3 %all-gather.2.cloned.1.call-done = f32[32768,128]{1,0:T(8,128)} async-done(((f32[2048,128]{1,0:T(8,128)}), f32[32768,128]{1,0:T(8,128)}) %all-gather.2.cloned.1.call-update) | async-done | bytes 16777232 | tf_op jit(solution)/shard_map/all_gather | solution.py:53
  114.2 6.4 %gather_fusion = f32[16,128,128]{2,1,0:T(8,128)S(1)} fusion(f32[256,128,128]{2,1,0:T(8,128)} %bitcast.119, s32[1024]{0:T(1024)S(1)} %pad_clamp_fusion), kind=kCustom, calls=%fused_computation | custom fusion | bytes 2097216 | tf_op jit(solution)/shard_map/gather | solution.py:54
  120.6 1.8 fusion
  122.4 1.8 convolution_bitcast_fusion.10
  124.2 1.8 convolution_bitcast_fusion.11
  126.1 211.4 %all-reduce.2.cloned.1.call-done = f32[128,128]{1,0:T(8,128)} async-done(((f32[128,128]{1,0:T(8,128)}), f32[128,128]{1,0:T(8,128)}) %all-reduce.2.cloned.1.call-update) | async-done | bytes 65552 | tf_op jit(solution)/shard_map/psum | solution.py:51
  337.5 1.2 fusion.12
  338.7 1.0 fusion.1
  339.7 1.8 convolution_bitcast_fusion.8
  341.5 1.1 multiply_reduce_fusion.5
  342.7 1.0 fusion.2
  343.7 1.8 convolution_bitcast_fusion.7
  345.5 1.1 multiply_reduce_fusion.3
  346.8 1.2 fusion.3
  347.9 1.8 convolution_bitcast_fusion.6
  349.8 1.1 multiply_reduce_fusion.1
  351.0 1.0 fusion.4
  352.0 1.8 convolution_bitcast_fusion.5
  354.2 0.7 copy.43
  (21 shorter events, 0.6 us)
Async XLA Ops:
  7.4 106.8 %all-gather.2.cloned.1.call-start = ((), (), s32[]{:S(2)}) async-start(), calls=%async_computation | async-start | bytes 17825792 | tf_op jit(solution)/shard_map/all_gather | solution.py:53
  8.1 329.4 %all-reduce.2.cloned.1.call-start = ((), (), s32[]{:S(2)}) async-start(), calls=%async_computation.1 | async-start | bytes 131072 | tf_op jit(solution)/shard_map/psum | solution.py:51
  337.5 16.3 %copy-start = (f32[128,128]{1,0:T(8,128)S(1)}, f32[128,128]{1,0:T(8,128)}, u32[]{:S(2)}) copy-start(f32[128,128]{1,0:T(8,128)} %all-reduce.2.cloned.1.call-done) | copy-start | bytes 196612
Sparse Core Ops, SparseCore 0:
  10.3 103.8 all-gather.1
Sparse Core Ops, SparseCore 1:
  13.6 323.9 all-reduce.1
where the time goes:
time: 363 us; the launch traced here: 362 us
  waiting for transfers between devices  313 us (86%)
  matrix products  23.5 us (6%)
  between operations  15 us (4%)
  local copies, waits for them, and re-layouts  9.38 us (3%)
    psum x1, waiting for transfers between devices, local(): gram = lax.psum(partial_gram, ('item', 'user'))  211 us
    all_gather x1, waiting for transfers between devices, local(): all_rows = lax.all_gather(item_factors, 'item', axis=0, tiled=True)  101 us
    dot_general x5, matrix products, apply_system(): jnp.einsum('bkui,bkir->bur', scores * weights, tiles, precision=HIGHEST)  9.1 us
  transfers between devices with their start and end apart: 2, of which 2 were waited for; matrix products, arithmetic and copies ran while one was open for 5% of the time, Pallas kernels for 0%

commit v1 on v0

--- a/solution.py
+++ b/solution.py
@@ -48,7 +48,7 @@
         item_factors, lax.axis_index("user") * share_rows, share_rows, 0
     )
     partial_gram = jnp.dot(piece.T, piece, precision=HIGHEST, preferred_element_type=jnp.float32)
-    gram = lax.psum(partial_gram, ("item", "user"))
+    gram = jnp.sum(lax.all_gather(partial_gram, axis_name=("item", "user")), axis=0)
     tile_ids = tile_lists.reshape(-1)
     all_rows = lax.all_gather(item_factors, "item", axis=0, tiled=True)
     fetched = all_rows.reshape(-1, tile_side, factor_rank)[tile_ids]

time: 363 us -> 311 us (0.86)
  waiting for transfers between devices: 313 us -> 254 us
  other arithmetic: 0.93 us -> 14.2 us
    psum x1 -> x0, waiting for transfers between devices: 211 us -> none  [local(): gram = lax.psum(partial_gram, ('item', 'user'))]
    all_gather x0 -> x1, waiting for transfers between devices: none -> 152 us  [local(): lax.all_gather(partial_gram, axis_name=('item', 'user'))]
    reduce_sum x0 -> x1, other arithmetic: none -> 13.3 us  [local(): jnp.sum(lax.all_gather(partial_gram, axis_name=('item', 'user')), axis=0)]
where the time goes in v1:
time: 311 us
  waiting for transfers between devices  254 us (82%)
  matrix products  19.9 us (6%)
  other arithmetic  14.2 us (5%)
  between operations  13.6 us (4%)
  local copies, waits for them, and re-layouts  9.36 us (3%)
    all_gather x1, waiting for transfers between devices, local(): lax.all_gather(partial_gram, axis_name=('item', 'user'))  152 us
    all_gather x1, waiting for transfers between devices, local(): all_rows = lax.all_gather(item_factors, 'item', axis=0, tiled=True)  101 us
    reduce_sum x1, other arithmetic, local(): jnp.sum(lax.all_gather(partial_gram, axis_name=('item', 'user')), axis=0)  13.3 us
    dot_general x5, matrix products, apply_system(): jnp.einsum('bkui,bkir->bur', scores * weights, tiles, precision=HIGHEST)  9.1 us
    gather x1, local copies, waits for them, and re-layouts, local(): fetched = all_rows.reshape(-1, tile_side, factor_rank)[tile_ids]  6.38 us
  transfers between devices with their start and end apart: 2, of which 2 were waited for; matrix products, arithmetic and copies ran while one was open for 5% of the time, Pallas kernels for 0%

profile of v1, /device:TPU:1, one launch (start us, length us, event | category | flops | bytes accessed | tf_op | source)
XLA Modules:
  0.0 310.7 jit_solution(3241352456686290061)
XLA Ops:
  6.5 0.7 all-gather.4.cloned.1.call-update
  7.3 1.8 fusion.22
  9.1 0.9 copy.33
  10.0 1.3 copy.24
  11.3 0.7 fusion.24
  12.0 101.0 %all-gather.4.cloned.1.call-done = f32[32768,128]{1,0:T(8,128)} async-done(((f32[2048,128]{1,0:T(8,128)}), f32[32768,128]{1,0:T(8,128)}) %all-gather.4.cloned.1.call-update) | async-done | bytes 16777232 | tf_op jit(solution)/shard_map/all_gather | solution.py:53
  113.0 6.4 %gather_fusion = f32[16,128,128]{2,1,0:T(8,128)S(1)} fusion(f32[256,128,128]{2,1,0:T(8,128)} %bitcast.121, s32[1024]{0:T(1024)S(1)} %pad_clamp_fusion), kind=kCustom, calls=%fused_computation | custom fusion | bytes 2097216 | tf_op jit(solution)/shard_map/gather | solution.py:54
  119.4 1.8 convolution_bitcast_fusion.11
  121.2 1.8 fusion
  123.1 1.8 convolution_bitcast_fusion.10
  124.9 151.9 %all-gather.6.cloned.1.call-done = f32[65536,128]{1,0:T(8,128)} async-done(((f32[128,128]{1,0:T(8,128)}), f32[65536,128]{1,0:T(8,128)}) %all-gather.6.cloned.1.call-update) | async-done | bytes 33554448 | tf_op jit(solution)/shard_map/all_gather | solution.py:51
  276.8 13.3 %reduce_sum.81 = f32[128,128]{1,0:T(8,128)S(1)} reduce(f32[512,128,128]{2,1,0:T(8,128)} %bitcast.120, f32[]{:T(128)} %constant.5.clone.1), dimensions={0}, to_apply=%region_0.0 | reduce | flops 8372224 | bytes 33619972 | tf_op jit(solution)/shard_map/reduce_sum | solution.py:51
  290.4 1.0 fusion.1
  291.4 1.8 convolution_bitcast_fusion.8
  293.2 0.3 multiply_reduce_fusion.5
  293.6 1.0 fusion.2
  294.6 1.8 convolution_bitcast_fusion.7
  296.4 0.3 multiply_reduce_fusion.3
  296.8 1.0 fusion.3
  297.8 1.8 convolution_bitcast_fusion.6
  299.6 0.3 multiply_reduce_fusion.1
  300.0 1.0 fusion.4
  301.0 1.8 convolution_bitcast_fusion.5
  303.1 0.7 copy.43
  (22 shorter events, 0.9 us)
Async XLA Ops:
  6.5 106.5 %all-gather.4.cloned.1.call-start = ((), (), s32[]{:S(2)}) async-start(), calls=%async_computation | async-start | bytes 17825792 | tf_op jit(solution)/shard_map/all_gather | solution.py:53
  7.3 269.5 %all-gather.6.cloned.1.call-start = ((), (), s32[]{:S(2)}) async-start(), calls=%async_computation.1 | async-start | bytes 33619968 | tf_op jit(solution)/shard_map/all_gather | solution.py:51
  276.8 13.3 %copy-start = (f32[128,128]{1,0:T(8,128)S(1)}, f32[128,128]{1,0:T(8,128)}, u32[]{:S(2)}) copy-start(f32[128,128]{1,0:T(8,128)} %param.7) | copy-start | bytes 196612
Sparse Core Ops, SparseCore 0:
  9.4 103.5 all-gather.3
  117.5 159.2 all-gather.5

commit v2 on v0

--- a/solution.py
+++ b/solution.py
@@ -48,7 +48,7 @@
         item_factors, lax.axis_index("user") * share_rows, share_rows, 0
     )
     partial_gram = jnp.dot(piece.T, piece, precision=HIGHEST, preferred_element_type=jnp.float32)
-    gram = lax.psum(partial_gram, ("item", "user"))
+    gram = jax.lax.psum(jax.lax.psum(partial_gram, "user"), "item")
     tile_ids = tile_lists.reshape(-1)
     all_rows = lax.all_gather(item_factors, "item", axis=0, tiled=True)
     fetched = all_rows.reshape(-1, tile_side, factor_rank)[tile_ids]

time: 363 us -> 299 us (0.82)
  waiting for transfers between devices: 313 us -> 250 us
    all_gather x1, waiting for transfers between devices: 101 us -> 0.03 us  [local(): all_rows = lax.all_gather(item_factors, 'item', axis=0, tiled=True)]
    psum x1 -> x2, waiting for transfers between devices: 211 us -> 249 us  [local(): gram = jax.lax.psum(jax.lax.psum(partial_gram, 'user'), 'item')]
  transfers between devices with their start and end apart: 2 -> 3, of which waited for: 2 -> 2; matrix products, arithmetic and copies ran while one was open for 5% -> 5% of each run, Pallas kernels for 0% -> 0%
where the time goes in v2:
time: 299 us
  waiting for transfers between devices  250 us (84%)
  matrix products  23.5 us (8%)
  between operations  15 us (5%)
  local copies, waits for them, and re-layouts  9.36 us (3%)
    psum x2, waiting for transfers between devices, local(): gram = jax.lax.psum(jax.lax.psum(partial_gram, 'user'), 'item')  249 us
    dot_general x5, matrix products, apply_system(): jnp.einsum('bkui,bkir->bur', scores * weights, tiles, precision=HIGHEST)  9.1 us
    gather x1, local copies, waits for them, and re-layouts, local(): fetched = all_rows.reshape(-1, tile_side, factor_rank)[tile_ids]  6.38 us
  transfers between devices with their start and end apart: 3, of which 2 were waited for; matrix products, arithmetic and copies ran while one was open for 5% of the time, Pallas kernels for 0%

profile of v2, /device:TPU:1, one launch (start us, length us, event | category | flops | bytes accessed | tf_op | source)
XLA Modules:
  0.0 298.6 jit_solution(94278415450173716)
XLA Ops:
  7.4 1.8 fusion.22
  9.2 0.5 all-gather.2.cloned.1.call-update
  9.8 1.3 copy.24
  11.1 0.9 copy.33
  12.0 0.7 fusion.24
  12.7 153.0 %all-reduce.3.cloned.1.call-done = f32[128,128]{1,0:T(8,128)} async-done(((f32[128,128]{1,0:T(8,128)}), f32[128,128]{1,0:T(8,128)}) %all-reduce.3.cloned.1.call-update) | async-done | bytes 65552 | tf_op jit(solution)/shard_map/psum | solution.py:51
  165.8 6.4 %gather_fusion = f32[16,128,128]{2,1,0:T(8,128)S(1)} fusion(f32[256,128,128]{2,1,0:T(8,128)} %bitcast.119, s32[1024]{0:T(1024)S(1)} %pad_clamp_fusion), kind=kCustom, calls=%fused_computation | custom fusion | bytes 2097216 | tf_op jit(solution)/shard_map/gather | solution.py:54
  172.2 1.8 fusion
  174.0 1.8 convolution_bitcast_fusion.10
  175.8 1.8 convolution_bitcast_fusion.11
  177.7 96.1 %all-reduce.5.cloned.1.call-done = f32[128,128]{1,0:T(8,128)} async-done(((f32[128,128]{1,0:T(8,128)}), f32[128,128]{1,0:T(8,128)}) %all-reduce.5.cloned.1.call-update) | async-done | bytes 65552 | tf_op jit(solution)/shard_map/psum | solution.py:51
  273.8 1.2 fusion.12
  275.0 1.0 fusion.1
  276.0 1.8 convolution_bitcast_fusion.8
  277.8 1.1 multiply_reduce_fusion.5
  279.0 1.0 fusion.2
  280.0 1.8 convolution_bitcast_fusion.7
  281.8 1.1 multiply_reduce_fusion.3
  283.1 1.2 fusion.3
  284.2 1.8 convolution_bitcast_fusion.6
  286.1 1.1 multiply_reduce_fusion.1
  287.3 1.0 fusion.4
  288.3 1.8 convolution_bitcast_fusion.5
  290.5 0.7 copy.43
  (24 shorter events, 0.7 us)
Async XLA Ops:
  7.4 158.4 %all-reduce.3.cloned.1.call-start = ((), (), s32[]{:S(2)}) async-start(), calls=%async_computation.1 | async-start | bytes 131072 | tf_op jit(solution)/shard_map/psum | solution.py:51
  9.1 156.6 %all-gather.2.cloned.1.call-start = ((), (), s32[]{:S(2)}) async-start(), calls=%async_computation | async-start | bytes 17825792 | tf_op jit(solution)/shard_map/all_gather | solution.py:53
  9.7 264.1 %all-reduce.5.cloned.1.call-start = ((), (), s32[]{:S(2)}) async-start(), calls=%async_computation.2 | async-start | bytes 131072 | tf_op jit(solution)/shard_map/psum | solution.py:51
  273.8 16.3 %copy-start = (f32[128,128]{1,0:T(8,128)S(1)}, f32[128,128]{1,0:T(8,128)}, u32[]{:S(2)}) copy-start(f32[128,128]{1,0:T(8,128)} %all-reduce.5.cloned.1.call-done) | copy-start | bytes 196612
Sparse Core Ops, SparseCore 0:
  11.6 154.0 all-reduce.2
Sparse Core Ops, SparseCore 1:
  11.7 103.5 all-gather.1
  165.8 107.9 all-reduce.4
